TPU v7x, 256 devices: a whole 4x4x8 slice. The times are simulated.
256 devices in a mesh: row: 16 (over y, z_lo), col: 16 (over x, z_hi, core).
Axes of the slice: x: 4, y: 4, z: 8 (z_hi: 2, z_lo: 4; z = z_hi * 4 + z_lo), core: 2. Of those that a mesh axis runs over, the one named last changes fastest.
Arguments:
- features: float32 [65536, 128], P(('col', 'row')), may hold values from -6 to 6
- weight: float32 [128, 128], replicated, may hold values from -4 to 4
- bias_vector: float32 [128], replicated, may hold values from -4 to 4
- out_grad: float32 [65536, 128], P(('row', 'col')), may hold values from -6 to 6
- adj_tiles: int32 [16, 16, 128, 128, 128], P('row', 'col'), may hold values 0 or 1
- tile_slots: int32 [16, 16, 128], P('row', 'col'), may hold values from 0 to 1023, as said below
- tile_counts: int32 [16, 16], P('row', 'col'), may hold values from 17 to 128, as said below
Outputs:
- activated: float32 [65536, 128], P(('row', 'col'))
- feature_grad: float32 [65536, 128], P(('col', 'row'))
- weight_grad: float32 [128, 128], replicated
- bias_grad: float32 [128], replicated
Inputs may be any that keep to these rules, and one draw needn't show every extreme that they name: `tile_slots`: each block's slots name distinct positions r * 32 + c of its 32 x 32 tiles. Some block is full in every draw; slots from tile_counts on are ignored.
All inputs are finite; a program needn't handle non-finite values. No bound on the sum of `adj_tiles` on one device may be relied on, other than what follows from the above.
Results may differ from a plain program's by a relative error of at most 0.0003.
Values sent between devices are 32-bit elements; how exact they have to be, the bound alone decides.
A program may use at most 128 MiB of HBM per device.

v0:
```python
import jax
import jax.numpy as jnp
from jax import lax
from jax.sharding import PartitionSpec as P

TILE = 128


def dense_step(aggregated, weight, bias_vector, cotangent):
    preact = jnp.dot(aggregated, weight, precision=lax.Precision.HIGHEST) + bias_vector
    logistic = jax.nn.sigmoid(preact)
    activated = preact * logistic
    pre_grad = cotangent * logistic * (1.0 + preact * (1.0 - logistic))
    weight_part = jnp.dot(aggregated.T, pre_grad, precision=lax.Precision.HIGHEST)
    bias_part = jnp.sum(pre_grad, axis=0)
    back_rows = jnp.dot(pre_grad, weight.T, precision=lax.Precision.HIGHEST)
    return (activated, weight_part, bias_part, back_rows)


def local(features, weight, bias_vector, out_grad, adj_tiles, tile_slots, tile_counts):
    row_count = lax.axis_size("row")
    col_count = lax.axis_size("col")
    node_rows = features.shape[0]
    width = features.shape[1]
    tile_rows = node_rows * col_count // TILE
    tile_cols = node_rows * row_count // TILE
    adjacency = adj_tiles[0, 0].astype(jnp.float32)
    slots = tile_slots[0, 0]
    slot_total = slots.shape[0]
    live_mask = (jnp.arange(slot_total) < tile_counts[0, 0]).astype(jnp.float32)
    tile_row = slots // tile_cols
    tile_col = slots % tile_cols
    row_select = (tile_row[:, None] == jnp.arange(tile_rows)[None, :]).astype(
        jnp.float32
    ) * live_mask[:, None]
    col_select = (tile_col[:, None] == jnp.arange(tile_cols)[None, :]).astype(
        jnp.float32
    ) * live_mask[:, None]
    dst_partial = jnp.dot(
        row_select.T, jnp.sum(adjacency, axis=2), precision=lax.Precision.HIGHEST
    ).reshape(-1)
    src_partial = jnp.dot(
        col_select.T, jnp.sum(adjacency, axis=1), precision=lax.Precision.HIGHEST
    ).reshape(-1)
    src_scale = lax.rsqrt(
        1.0 + lax.psum_scatter(src_partial, "row", scatter_dimension=0, tiled=True)
    )
    scaled = features * src_scale[:, None]
    gathered = lax.all_gather(scaled, "row", axis=0, tiled=True)
    taken = jnp.take(gathered.reshape(tile_cols, TILE, width), tile_col, axis=0)
    product = jnp.einsum(
        "kab,kbh->kah",
        adjacency,
        taken,
        precision=lax.Precision.HIGHEST,
        preferred_element_type=jnp.float32,
    )
    partial_value = jnp.einsum(
        "kr,kah->rah",
        row_select,
        product,
        precision=lax.Precision.HIGHEST,
        preferred_element_type=jnp.float32,
    ).reshape(tile_rows * TILE, width)
    dst_scale = lax.rsqrt(
        1.0 + lax.psum_scatter(dst_partial, "col", scatter_dimension=0, tiled=True)
    )
    aggregated = (
        lax.psum_scatter(partial_value, "col", scatter_dimension=0, tiled=True) * dst_scale[:, None]
    )
    activated, weight_part, bias_part, back_rows = dense_step(
        aggregated, weight, bias_vector, out_grad
    )
    weight_grad, bias_grad = lax.psum((weight_part, bias_part), ("row", "col"))
    row_grads = lax.all_gather(back_rows * dst_scale[:, None], "col", axis=0, tiled=True)
    taken_back = jnp.take(row_grads.reshape(tile_rows, TILE, width), tile_row, axis=0)
    product_back = jnp.einsum(
        "kab,kah->kbh",
        adjacency,
        taken_back,
        precision=lax.Precision.HIGHEST,
        preferred_element_type=jnp.float32,
    )
    partial_back = jnp.einsum(
        "kc,kbh->cbh",
        col_select,
        product_back,
        precision=lax.Precision.HIGHEST,
        preferred_element_type=jnp.float32,
    ).reshape(tile_cols * TILE, width)
    feature_grad = (
        lax.psum_scatter(partial_back, "row", scatter_dimension=0, tiled=True) * src_scale[:, None]
    )
    return (activated, feature_grad, weight_grad, bias_grad)


def solution(mesh):
    return jax.shard_map(
        local,
        mesh=mesh,
        in_specs=(
            P(("col", "row"), None),
            P(),
            P(),
            P(("row", "col"), None),
            P("row", "col", None, None, None),
            P("row", "col", None),
            P("row", "col"),
        ),
        out_specs=(P(("row", "col"), None), P(("col", "row"), None), P(), P()),
        check_vma=False,
    )
```

profile of v0, /device:TPU:1, one launch (start us, length us, event | category | flops | bytes accessed | tf_op | source)
XLA Modules:
  0.0 764.2 jit_solution(688655162839533169)
XLA Ops:
  7.9 1.3 dynamic-slice
  9.9 5.7 convert_reduce_fusion
  15.8 68.3 %all-reduce = f32[4096]{0:T(1024)S(1)} all-reduce(f32[4096]{0:T(1024)S(1)} %convolution_bitcast_fusion.1), channel_id=2, replica_groups=mesh['row'=16,'col'=16] {'row'}, use_global_device_ids=true, to_apply=%region_1.2.clone | all-reduce | flops 4096 | bytes 32768
  85.1 89.2 %all-gather.3.cloned.1.call-done = f32[4096,128]{1,0:T(8,128)} async-done(((f32[256,128]{1,0:T(8,128)}), f32[4096,128]{1,0:T(8,128)}) %all-gather.3.cloned.1.call-update) | async-done | bytes 2097168 | tf_op jit(solution)/shard_map/all_gather | solution.py:49
  174.3 5.9 gather_fusion
  180.1 21.5 %fusion.12 = f32[128,128,128]{1,2,0:T(8,128)} fusion(s32[1,1,128,128,128]{4,3,2,1,0:T(8,128)} %param.13, f32[128,128,128]{2,1,0:T(8,128)} %gather_fusion, pred[128]{0:T(512)(128)(4,1)S(1)} %get-tuple-element.14), kind=kOutput, calls=%fused_computation.16 | convolution fusion | flops 3225419776 | bytes 25165952 | tf_op jit(solution)/shard_map/kab,kbh->kah/dot_general | solution.py:51
  201.7 9.3 %copy.18 = f32[128,128,128]{2,0,1:T(8,128)} copy(f32[128,128,128]{1,2,0:T(8,128)} %fusion.12) | data formatting | bytes 16777216 | tf_op jit(solution)/shard_map/kab,kbh->kah/dot_general | solution.py:51
  211.0 6.8 fusion.30
  217.7 2.6 copy.19
  221.8 87.6 %all-reduce.1 = f32[4096]{0:T(1024)S(1)} all-reduce(f32[4096]{0:T(1024)S(1)} %convolution_bitcast_fusion), channel_id=4, replica_groups=mesh['row'=16,'col'=16] {'col'}, use_global_device_ids=true, to_apply=%region_4.6.clone | all-reduce | flops 4096 | bytes 32768
  309.5 4.8 reduce-scatter.3.cloned.1.call-done
  314.3 1.9 fusion.52
  316.2 0.9 convolution_multiply_fusion
  317.2 62.5 %all-gather.5.cloned.1.call-done = f32[4096,128]{1,0:T(8,128)} async-done(((f32[256,128]{1,0:T(8,128)}), f32[4096,128]{1,0:T(8,128)}) %all-gather.5.cloned.1.call-update) | async-done | bytes 2097168 | tf_op jit(solution)/shard_map/all_gather | solution.py:75
  379.7 5.9 gather_fusion.1
  385.6 19.7 %fusion.17 = f32[128,128,128]{1,2,0:T(8,128)} fusion(s32[1,1,128,128,128]{4,3,2,1,0:T(8,128)} %param.13, f32[128,128,128]{2,1,0:T(8,128)} %gather_fusion.1, pred[128]{0:T(512)(128)(4,1)S(1)} %get-tuple-element.9), kind=kOutput, calls=%fused_computation.17 | convolution fusion | flops 3225419776 | bytes 25165952 | tf_op jit(solution)/shard_map/kab,kah->kbh/dot_general | solution.py:77
  405.3 9.3 %copy.21 = f32[128,128,128]{2,0,1:T(8,128)} copy(f32[128,128,128]{1,2,0:T(8,128)} %fusion.17) | data formatting | bytes 16777216 | tf_op jit(solution)/shard_map/kab,kah->kbh/dot_general | solution.py:77
  414.6 6.8 fusion.31
  421.4 2.6 copy.22
  424.0 76.6 %psum.15 = f32[128]{0:T(128)} all-reduce(f32[128]{0:T(128)S(1)} %get-tuple-element.7), channel_id=1, replica_groups=mesh['row'=16,'col'=16] {'row','col'}, use_global_device_ids=true, to_apply=%region_8.10 | all-reduce | flops 128 | bytes 1024 | tf_op jit(solution)/shard_map/psum | solution.py:74
  500.6 1.1 fusion.23
  501.8 1.7 broadcast_multiply_fusion
  503.4 252.8 %all-reduce.4.cloned.1.call-done = f32[128,128]{1,0:T(8,128)} async-done(((f32[128,128]{1,0:T(8,128)}), f32[128,128]{1,0:T(8,128)}) %all-reduce.4.cloned.1.call-update) | async-done | bytes 65552 | tf_op jit(solution)/shard_map/psum | solution.py:74
  756.2 1.5 copy.27
  (36 shorter events, 2.2 us)
Async XLA Ops:
  7.2 307.1 %copy-start = (f32[128,128]{1,0:T(8,128)S(1)}, f32[128,128]{1,0:T(8,128)}, u32[]{:S(2)}) copy-start(f32[128,128]{1,0:T(8,128)} %param.10) | copy-start | bytes 196612
  7.2 8.4 %copy-start.3 = (s32[1,1,128]{2,1,0:T(1,128)S(1)}, s32[1,1,128]{2,1,0:T(1,128)}, u32[]{:S(2)}) copy-start(s32[1,1,128]{2,1,0:T(1,128)} %param.14) | copy-start | bytes 1540
  7.2 77.0 %copy-start.1 = (f32[256,128]{1,0:T(8,128)S(1)}, f32[256,128]{1,0:T(8,128)}, u32[]{:S(2)}) copy-start(f32[256,128]{1,0:T(8,128)} %param.9) | copy-start | bytes 393220
  7.2 167.1 %all-gather.3.cloned.1.call-start = ((), (), s32[]{:S(2)}) async-start(), calls=%async_computation.2 | async-start | bytes 2228224 | tf_op jit(solution)/shard_map/all_gather | solution.py:49
  85.0 229.3 %reduce-scatter.3.cloned.1.call-start = ((), (), s32[]{:S(2)}) async-start(), calls=%async_computation.3 | async-start | bytes 2228224 | tf_op jit(solution)/shard_map/reduce_scatter | solution.py:69
  211.0 9.4 %copy-start.6 = (u32[256]{0:T(256)S(1)}, u32[256]{0:T(256)}, u32[]{:S(2)}) copy-start(u32[256]{0:T(256)} %constant.56) | copy-start | bytes 3076
  211.0 103.3 %copy-start.4 = (f32[256,128]{1,0:T(8,128)S(1)}, f32[256,128]{1,0:T(8,128)}, u32[]{:S(2)}) copy-start(f32[256,128]{1,0:T(8,128)} %param.12) | copy-start | bytes 393220
  211.0 103.3 %copy-start.5 = (f32[128]{0:T(128)S(1)}, f32[128]{0:T(128)}, u32[]{:S(2)}) copy-start(f32[128]{0:T(128)} %param.11) | copy-start | bytes 1540
  220.3 159.4 %all-gather.5.cloned.1.call-start = ((), (), s32[]{:S(2)}) async-start(), calls=%async_computation.4 | async-start | bytes 2228224 | tf_op jit(solution)/shard_map/all_gather | solution.py:75
  317.2 184.6 %reduce-scatter.5.cloned.1.call-start = ((), (), s32[]{:S(2)}) async-start(), calls=%async_computation.5 | async-start | bytes 2228224 | tf_op jit(solution)/shard_map/reduce_scatter | solution.py:92
  414.6 86.0 %copy-start.2 = (f32[256,128]{1,0:T(8,128)S(1)}, f32[256,128]{1,0:T(8,128)}, u32[]{:S(2)}) copy-start(f32[256,128]{1,0:T(8,128)} %reduce-scatter.3.cloned.1.call-done) | copy-start | bytes 393220
  424.0 332.2 %all-reduce.4.cloned.1.call-start = ((), (), s32[]{:S(2)}) async-start(), calls=%async_computation.6 | async-start | bytes 131072 | tf_op jit(solution)/shard_map/psum | solution.py:74
Sparse Core Ops, SparseCore 0:
  85.1 89.0 all-gather.2
  220.5 93.7 reduce-scatter.2
  317.5 62.1 all-gather.4
  424.1 77.1 reduce-scatter.4
  507.3 248.8 all-reduce.3
where the time goes:
time: 765 us; the launch traced here: 764 us
  waiting for transfers between devices  409 us (53%)
  blocking collectives  232 us (30%)
  matrix products  59 us (8%)
  local copies, waits for them, and re-layouts  38.9 us (5%)
  between operations  15.9 us (2%)
  other arithmetic  8.34 us (1%)
    psum x1, waiting for transfers between devices, local(): weight_grad, bias_grad = lax.psum((weight_part, bias_part), ('row', 'col'))  253 us
    unnamed x2, blocking collectives  156 us
    all_gather x1, waiting for transfers between devices, local(): gathered = lax.all_gather(scaled, 'row', axis=0, tiled=True)  89.2 us
    psum x1, blocking collectives, local(): weight_grad, bias_grad = lax.psum((weight_part, bias_part), ('row', 'col'))  76.6 us
    all_gather x1, waiting for transfers between devices, local(): lax.all_gather(back_rows * dst_scale[:, None], 'col', axis=0, tiled=True)  62.5 us
    dot_general x1, matrix products, local(): jnp.einsum('kab,kbh->kah', adjacency, taken, precision=lax.Precision.HIGH...  21.5 us
    dot_general x1, matrix products, local(): jnp.einsum('kab,kah->kbh', adjacency, taken_back, precision=lax.Precision...  19.7 us
  transfers between devices with their start and end apart: 5, of which 4 were waited for; matrix products, arithmetic and copies ran while one was open for 0% of the time, Pallas kernels for 0%

commit v1 on v0

--- a/solution.py
+++ b/solution.py
@@ -71,7 +71,7 @@
     activated, weight_part, bias_part, back_rows = dense_step(
         aggregated, weight, bias_vector, out_grad
     )
-    weight_grad, bias_grad = lax.psum((weight_part, bias_part), ("row", "col"))
+    weight_grad, bias_grad = lax.psum(lax.psum((weight_part, bias_part), "col"), "row")
     row_grads = lax.all_gather(back_rows * dst_scale[:, None], "col", axis=0, tiled=True)
     taken_back = jnp.take(row_grads.reshape(tile_rows, TILE, width), tile_row, axis=0)
     product_back = jnp.einsum(

time: 765 us -> 795 us (1.039); the launches traced: 764 us -> 786 us
  waiting for transfers between devices: 409 us -> 430 us
    reduce_scatter x1, waiting for transfers between devices: 0.02 us -> 84 us  [local(): lax.psum_scatter(partial_back, 'row', scatter_dimension=0, tiled=True)]
    psum x1 -> x2, waiting for transfers between devices: 253 us -> 192 us  [the longest x1 148 us: local(): lax.psum(lax.psum((weight_part, bias_part), 'col'), 'row')]
    psum x1 -> x2, blocking collectives: 76.6 us -> 76 us  [the longest x1 42.4 us: local(): lax.psum((weight_part, bias_part), 'col')]
  transfers between devices with their start and end apart: 5 -> 6, of which waited for: 4 -> 6; matrix products, arithmetic and copies ran while one was open for 0% -> 6% of each run, Pallas kernels for 0% -> 0%
where the time goes in v1:
time: 795 us; the launch traced here: 786 us
  waiting for transfers between devices  430 us (54%)
  blocking collectives  232 us (29%)
  matrix products  59.9 us (8%)
  local copies, waits for them, and re-layouts  38.9 us (5%)
  between operations  16.2 us (2%)
  other arithmetic  8.34 us (1%)
    unnamed x2, blocking collectives  156 us
    psum x1, waiting for transfers between devices, local(): lax.psum(lax.psum((weight_part, bias_part), 'col'), 'row')  148 us
    all_gather x1, waiting for transfers between devices, local(): gathered = lax.all_gather(scaled, 'row', axis=0, tiled=True)  89.2 us
    reduce_scatter x1, waiting for transfers between devices, local(): lax.psum_scatter(partial_back, 'row', scatter_dimension=0, tiled=True)  84 us
    all_gather x1, waiting for transfers between devices, local(): lax.all_gather(back_rows * dst_scale[:, None], 'col', axis=0, tiled=True)  60 us
    psum x1, waiting for transfers between devices, local(): lax.psum((weight_part, bias_part), 'col')  44 us
    psum x1, blocking collectives, local(): lax.psum((weight_part, bias_part), 'col')  42.4 us
    psum x1, blocking collectives, local(): lax.psum(lax.psum((weight_part, bias_part), 'col'), 'row')  33.6 us
  transfers between devices with their start and end apart: 6, of which 6 were waited for; matrix products, arithmetic and copies ran while one was open for 6% of the time, Pallas kernels for 0%

profile of v1, /device:TPU:1, one launch (start us, length us, event | category | flops | bytes accessed | tf_op | source)
XLA Modules:
  0.0 785.9 jit_solution(5417639628907981225)
XLA Ops:
  9.9 5.7 convert_reduce_fusion
  15.8 68.3 %all-reduce = f32[4096]{0:T(1024)S(1)} all-reduce(f32[4096]{0:T(1024)S(1)} %convolution_bitcast_fusion.1), channel_id=2, replica_groups=mesh['row'=16,'col'=16] {'row'}, use_global_device_ids=true, to_apply=%region_1.2.clone | all-reduce | flops 4096 | bytes 32768
  85.1 89.2 %all-gather.3.cloned.1.call-done = f32[4096,128]{1,0:T(8,128)} async-done(((f32[256,128]{1,0:T(8,128)}), f32[4096,128]{1,0:T(8,128)}) %all-gather.3.cloned.1.call-update) | async-done | bytes 2097168 | tf_op jit(solution)/shard_map/all_gather | solution.py:49
  174.3 5.9 gather_fusion
  180.1 21.5 %fusion.12 = f32[128,128,128]{1,2,0:T(8,128)} fusion(s32[1,1,128,128,128]{4,3,2,1,0:T(8,128)} %param.13, f32[128,128,128]{2,1,0:T(8,128)} %gather_fusion, pred[128]{0:T(512)(128)(4,1)S(1)} %get-tuple-element.14), kind=kOutput, calls=%fused_computation.16 | convolution fusion | flops 3225419776 | bytes 25165952 | tf_op jit(solution)/shard_map/kab,kbh->kah/dot_general | solution.py:51
  201.7 9.3 %copy.18 = f32[128,128,128]{2,0,1:T(8,128)} copy(f32[128,128,128]{1,2,0:T(8,128)} %fusion.12) | data formatting | bytes 16777216 | tf_op jit(solution)/shard_map/kab,kbh->kah/dot_general | solution.py:51
  211.0 6.8 fusion.30
  217.8 2.6 copy.19
  221.8 87.6 %all-reduce.1 = f32[4096]{0:T(1024)S(1)} all-reduce(f32[4096]{0:T(1024)S(1)} %convolution_bitcast_fusion), channel_id=4, replica_groups=mesh['row'=16,'col'=16] {'col'}, use_global_device_ids=true, to_apply=%region_4.6.clone | all-reduce | flops 4096 | bytes 32768
  309.5 5.2 reduce-scatter.3.cloned.1.call-done
  314.7 1.9 fusion.52
  317.7 2.0 fusion.23
  319.8 60.0 %all-gather.5.cloned.1.call-done = f32[4096,128]{1,0:T(8,128)} async-done(((f32[256,128]{1,0:T(8,128)}), f32[4096,128]{1,0:T(8,128)}) %all-gather.5.cloned.1.call-update) | async-done | bytes 2097168 | tf_op jit(solution)/shard_map/all_gather | solution.py:75
  379.7 5.9 gather_fusion.1
  385.6 19.7 %fusion.17 = f32[128,128,128]{1,2,0:T(8,128)} fusion(s32[1,1,128,128,128]{4,3,2,1,0:T(8,128)} %param.13, f32[128,128,128]{2,1,0:T(8,128)} %gather_fusion.1, pred[128]{0:T(512)(128)(4,1)S(1)} %get-tuple-element.9), kind=kOutput, calls=%fused_computation.17 | convolution fusion | flops 3225419776 | bytes 25165952 | tf_op jit(solution)/shard_map/kab,kah->kbh/dot_general | solution.py:77
  405.4 9.3 %copy.21 = f32[128,128,128]{2,0,1:T(8,128)} copy(f32[128,128,128]{1,2,0:T(8,128)} %fusion.17) | data formatting | bytes 16777216 | tf_op jit(solution)/shard_map/kab,kah->kbh/dot_general | solution.py:77
  414.7 6.7 fusion.31
  421.4 2.6 copy.22
  424.0 42.4 %psum.30 = f32[128]{0:T(128)S(1)} all-reduce(f32[128]{0:T(128)S(1)} %get-tuple-element.7), channel_id=1, replica_groups=mesh['row'=16,'col'=16] {'col'}, use_global_device_ids=true, to_apply=%region_9.11 | all-reduce | flops 128 | bytes 1024 | tf_op jit(solution)/shard_map/psum | solution.py:74
  466.5 33.6 %psum.31 = f32[128]{0:T(128)} all-reduce(f32[128]{0:T(128)S(1)} %psum.30), channel_id=1, replica_groups=mesh['row'=16,'col'=16] {'row'}, use_global_device_ids=true, to_apply=%region_10.12 | all-reduce | flops 128 | bytes 1024 | tf_op jit(solution)/shard_map/psum | solution.py:74
  500.0 44.0 %all-reduce.5.cloned.1.call-done = f32[128,128]{1,0:T(8,128)} async-done(((f32[128,128]{1,0:T(8,128)}), f32[128,128]{1,0:T(8,128)}) %all-reduce.5.cloned.1.call-update) | async-done | bytes 65552 | tf_op jit(solution)/shard_map/psum | solution.py:74
  544.1 84.0 %reduce-scatter.5.cloned.1.call-done = f32[256,128]{1,0:T(8,128)} async-done(((f32[4096,128]{1,0:T(8,128)}), f32[256,128]{1,0:T(8,128)}) %reduce-scatter.5.cloned.1.call-update) | async-done | bytes 131088 | tf_op jit(solution)/shard_map/reduce_scatter | solution.py:92
  628.1 1.7 broadcast_multiply_fusion
  629.8 147.8 %all-reduce.7.cloned.1.call-done = f32[128,128]{1,0:T(8,128)} async-done(((f32[128,128]{1,0:T(8,128)}), f32[128,128]{1,0:T(8,128)}) %all-reduce.7.cloned.1.call-update) | async-done | bytes 65552 | tf_op jit(solution)/shard_map/psum | solution.py:74
  (38 shorter events, 5.9 us)
Async XLA Ops:
  7.2 307.6 %copy-start = (f32[128,128]{1,0:T(8,128)S(1)}, f32[128,128]{1,0:T(8,128)}, u32[]{:S(2)}) copy-start(f32[128,128]{1,0:T(8,128)} %param.10) | copy-start | bytes 196612
  7.2 8.4 %copy-start.2 = (s32[1,1,128]{2,1,0:T(1,128)S(1)}, s32[1,1,128]{2,1,0:T(1,128)}, u32[]{:S(2)}) copy-start(s32[1,1,128]{2,1,0:T(1,128)} %param.14) | copy-start | bytes 1540
  7.2 77.0 %copy-start.1 = (f32[256,128]{1,0:T(8,128)S(1)}, f32[256,128]{1,0:T(8,128)}, u32[]{:S(2)}) copy-start(f32[256,128]{1,0:T(8,128)} %param.9) | copy-start | bytes 393220
  7.2 167.1 %all-gather.3.cloned.1.call-start = ((), (), s32[]{:S(2)}) async-start(), calls=%async_computation.2 | async-start | bytes 2228224 | tf_op jit(solution)/shard_map/all_gather | solution.py:49
  85.0 229.7 %reduce-scatter.3.cloned.1.call-start = ((), (), s32[]{:S(2)}) async-start(), calls=%async_computation.3 | async-start | bytes 2228224 | tf_op jit(solution)/shard_map/reduce_scatter | solution.py:69
  211.0 9.4 %copy-start.5 = (u32[256]{0:T(256)S(1)}, u32[256]{0:T(256)}, u32[]{:S(2)}) copy-start(u32[256]{0:T(256)} %constant.56) | copy-start | bytes 3076
  211.0 103.7 %copy-start.3 = (f32[256,128]{1,0:T(8,128)S(1)}, f32[256,128]{1,0:T(8,128)}, u32[]{:S(2)}) copy-start(f32[256,128]{1,0:T(8,128)} %param.12) | copy-start | bytes 393220
  211.0 103.7 %copy-start.4 = (f32[128]{0:T(128)S(1)}, f32[128]{0:T(128)}, u32[]{:S(2)}) copy-start(f32[128]{0:T(128)} %param.11) | copy-start | bytes 1540
  220.3 159.4 %all-gather.5.cloned.1.call-start = ((), (), s32[]{:S(2)}) async-start(), calls=%async_computation.4 | async-start | bytes 2228224 | tf_op jit(solution)/shard_map/all_gather | solution.py:75
  317.6 226.5 %all-reduce.5.cloned.1.call-start = ((), (), s32[]{:S(2)}) async-start(), calls=%async_computation.6 | async-start | bytes 131072 | tf_op jit(solution)/shard_map/psum | solution.py:74
  319.7 308.4 %reduce-scatter.5.cloned.1.call-start = ((), (), s32[]{:S(2)}) async-start(), calls=%async_computation.5 | async-start | bytes 2228224 | tf_op jit(solution)/shard_map/reduce_scatter | solution.py:92
  424.0 353.6 %all-reduce.7.cloned.1.call-start = ((), (), s32[]{:S(2)}) async-start(), calls=%async_computation.7 | async-start | bytes 131072 | tf_op jit(solution)/shard_map/psum | solution.py:74
Sparse Core Ops, SparseCore 0:
  85.1 89.0 all-gather.2
  220.5 94.2 reduce-scatter.2
  318.0 61.7 all-gather.4
  382.8 161.2 all-reduce.4
  546.5 81.5 reduce-scatter.4
  630.6 146.9 all-reduce.6
